TPU v7x, 256 devices: a whole 4x4x8 slice. The times are simulated.
256 devices in a mesh: dp: 16 (over z, core), tensor: 16 (over x, y).
Axes of the slice: x: 4, y: 4, z: 8, core: 2. Of those that a mesh axis runs over, the one named last changes fastest.
Arguments:
- inputs: bfloat16 [4096, 6144], P('dp'), may hold values from -6 to 6
- grad_hidden: bfloat16 [4096, 24576], P('dp', 'tensor'), may hold values from -6 to 6
- w_blocks: bfloat16 [16, 288, 128, 128], P('tensor', 'dp'), may hold values from -0.15625 to 0.15625
- block_ids: int32 [16, 288], P('tensor', 'dp'), may hold values from 0 to 575, as said below
- counts: int32 [16, 16], P('tensor', 'dp'), may hold values from 1 to 18, 144 in all within a row
Outputs:
- hidden: bfloat16 [4096, 24576], P('dp', 'tensor')
- grad_inputs: bfloat16 [4096, 6144], P('dp', 'tensor')
- grad_blocks: bfloat16 [16, 288, 128, 128], P('tensor', 'dp')
Inputs may be any that keep to these rules, and one draw needn't show every extreme that they name: `block_ids`: within one tensor index all 288 ids are distinct. Each row of counts sums to 144.
All inputs are finite; a program needn't handle non-finite values. No bound on the sum of `counts` on one device may be relied on, other than what follows from the above.
Results may differ from a plain program's by a relative error of at most 0.023.
Values may be sent and summed in bfloat16 or wider, within the bound.
A program may use at most 128 MiB of HBM per device.

v0:
```python
import math
import jax
import jax.numpy as jnp
from jax import lax
from jax.sharding import PartitionSpec as P

GELU_C = 0.7978845608028654
GELU_A = 0.044715


def gelu_value(values):
    inner_arg = GELU_C * (values + GELU_A * values * values * values)
    return 0.5 * values * (1.0 + jnp.tanh(inner_arg))


def gelu_slope(values):
    inner_arg = GELU_C * (values + GELU_A * values * values * values)
    tanh_value = jnp.tanh(inner_arg)
    return 0.5 * (1.0 + tanh_value) + 0.5 * values * (1.0 - tanh_value * tanh_value) * GELU_C * (
        1.0 + 3.0 * GELU_A * values * values
    )


def select_live(gathered, capacity, col_blocks):
    blocks = gathered[0][0]
    ids_row = gathered[1][0]
    owner_counts = gathered[2][0]
    slot_total = ids_row.shape[0]
    live_total = slot_total // 2
    slot_index = jnp.arange(slot_total, dtype=jnp.int32)
    is_live = slot_index % capacity < owner_counts[slot_index // capacity]
    live_order = jnp.argsort(jnp.where(is_live, 0, 1).astype(jnp.int32), stable=True)[:live_total]
    live_ids = ids_row[live_order]
    block_size = blocks.shape[-1]
    grouped = (
        blocks[live_order].reshape(live_total // 16, 16, block_size, block_size),
        (live_ids // col_blocks).reshape(live_total // 16, 16),
        (live_ids % col_blocks).reshape(live_total // 16, 16),
    )
    return (grouped, live_order)


def one_hot(indices, length, dtype):
    return (indices[:, None] == jnp.arange(length, dtype=jnp.int32)[None, :]).astype(dtype)


def per_device(inputs, grad_hidden, w_blocks, block_ids, counts):
    tok_rows, model_width = inputs.shape
    block_size = w_blocks.shape[-1]
    row_blocks = model_width // block_size
    capacity = w_blocks.shape[1]
    col_blocks = grad_hidden.shape[1] // block_size
    group_count = lax.axis_size("dp")
    x_blocks = inputs.reshape(tok_rows, row_blocks, block_size)
    gathered = (
        lax.all_gather(w_blocks, "dp", axis=1, tiled=True),
        lax.all_gather(block_ids, "dp", axis=1, tiled=True),
        lax.all_gather(counts, "dp", axis=1, tiled=True),
    )
    forward_pieces, forward_order = select_live(gathered, capacity, col_blocks)

    def pick_rows(rows_here):
        rows_hot = one_hot(rows_here, row_blocks, jnp.bfloat16)
        return jnp.einsum(
            "trb,gr->tgb", x_blocks, rows_hot, preferred_element_type=jnp.float32
        ).astype(jnp.bfloat16)

    def forward_group(running, group_data):
        block_piece, rows_here, cols_here = group_data
        x_rows = pick_rows(rows_here)
        product = jnp.einsum(
            "tgb,gbc->tgc", x_rows, block_piece, preferred_element_type=jnp.float32
        )
        cols_hot = one_hot(cols_here, col_blocks, jnp.float32)
        placed = jnp.einsum("tgc,gk->tkc", product, cols_hot, precision=lax.Precision.HIGHEST)
        return (running + placed, None)

    pre_three, unused = lax.scan(
        forward_group, jnp.zeros((tok_rows, col_blocks, block_size), jnp.float32), forward_pieces
    )
    pre_act = pre_three.reshape(tok_rows, col_blocks * block_size)
    hidden = gelu_value(pre_act).astype(jnp.bfloat16)
    grad_pre = (grad_hidden.astype(jnp.float32) * gelu_slope(pre_act)).astype(jnp.bfloat16)
    grad_three = grad_pre.reshape(tok_rows, col_blocks, block_size)
    backward_pieces, backward_order = (forward_pieces, forward_order)

    def backward_group(running, group_data):
        block_piece, rows_here, cols_here = group_data
        cols_pick = one_hot(cols_here, col_blocks, jnp.bfloat16)
        grad_piece = jnp.einsum(
            "tkc,gk->tgc", grad_three, cols_pick, preferred_element_type=jnp.float32
        ).astype(jnp.bfloat16)
        contrib = jnp.einsum(
            "tgc,gbc->tgb", grad_piece, block_piece, preferred_element_type=jnp.float32
        )
        x_rows = pick_rows(rows_here)
        weight_part = jnp.einsum(
            "tgb,tgc->gbc", x_rows, grad_piece, preferred_element_type=jnp.float32
        )
        rows_place = one_hot(rows_here, row_blocks, jnp.float32)
        placed = jnp.einsum("tgb,gr->trb", contrib, rows_place, precision=lax.Precision.HIGHEST)
        return (running + placed, weight_part)

    input_three, weight_parts = lax.scan(
        backward_group, jnp.zeros((tok_rows, row_blocks, block_size), jnp.float32), backward_pieces
    )
    live_total = backward_order.shape[0]
    weight_parts = weight_parts.reshape(live_total, block_size, block_size)
    grad_inputs = lax.psum_scatter(
        input_three.reshape(tok_rows, model_width).astype(jnp.bfloat16),
        "tensor",
        scatter_dimension=1,
        tiled=True,
    )
    position = (
        jnp.full((capacity * group_count,), -1, jnp.int32)
        .at[backward_order]
        .set(jnp.arange(live_total, dtype=jnp.int32))
    )
    grad_scale = 1.0 / math.sqrt(tok_rows * group_count)
    picked = weight_parts[jnp.maximum(position, 0)]
    summed = lax.psum_scatter(
        jnp.where((position >= 0)[:, None, None], picked, 0.0).astype(jnp.bfloat16),
        "dp",
        scatter_dimension=0,
        tiled=True,
    ).astype(jnp.float32)
    grad_blocks = (summed * grad_scale).astype(jnp.bfloat16)[None]
    return (hidden, grad_inputs, grad_blocks)


def solution(mesh):
    in_specs = (
        P("dp", None),
        P("dp", "tensor"),
        P("tensor", "dp", None, None),
        P("tensor", "dp"),
        P("tensor", "dp"),
    )
    out_specs = (P("dp", "tensor"), P("dp", "tensor"), P("tensor", "dp", None, None))
    return jax.shard_map(
        per_device, mesh=mesh, in_specs=in_specs, out_specs=out_specs, check_vma=False
    )
```

profile of v0, /device:TPU:6, one launch (start us, length us, event | category | flops | bytes accessed | tf_op | source)
XLA Modules:
  0.0 545.4 jit_solution(3201787974582969719)
XLA Ops:
  12.0 16.4 %all-reduce.2 = (s32[288]{0:T(512)S(1)}, s32[16]{0:T(128)S(1)}) all-reduce(s32[288]{0:T(512)S(1)} %bitcast_dynamic-update-slice_fusion.1, s32[16]{0:T(128)S(1)} %bitcast_dynamic-update-slice_fusion), channel_id=1, replica_groups=mesh['dp'=16,'tensor'=16] {'dp'}, use_global_device_ids=true, to_apply=%add | all-reduce | flops 304 | bytes 2432 | tf_op jit(solution)/shard_map/squeeze | solution.py:26
  33.9 5.5 %fusion.44 = s32[288]{0:T(512)S(1)} fusion(pred[288]{0:T(512)(128)(4,1)S(1)} %compare_reduce_fusion, pred[288]{0:T(512)(128)(4,1)S(1)} %compare_reduce_fusion.1, pred[288]{0:T(512)(128)(4,1)S(1)} %compare_reduce_fusion.2, pred[288]{0:T(512)(128)(4,1)S(1)} %compare_reduce_fusion.3, pred[288]{0:T(512)(128)(4,1)S(1)} %compare_reduce_fusion.4, ...), kind=kLoop, calls=%fused_computation.93 | loop fusion | flops 4896 | bytes 4932 | tf_op jit(solution)/shard_map/jit(_where)/select_n | solution.py:32
  50.2 23.5 %all-gather.2.cloned.1.call-done = bf16[1,288,128,128]{3,2,0,1:T(8,128)(2,1)} async-done(((bf16[1,18,128,128]{3,2,0,1:T(8,128)(2,1)}), bf16[1,288,128,128]{3,2,0,1:T(8,128)(2,1)}) %all-gather.2.cloned.1.call-update) | async-done | bytes 9437200 | tf_op jit(solution)/shard_map/all_gather | solution.py:56
  73.7 11.2 %gather_fusion.1 = bf16[144,128,128]{2,1,0:T(8,128)(2,1)} fusion(bf16[288,128,128]{2,1,0:T(8,128)(2,1)} %bitcast.149, s32[1024]{0:T(1024)S(1)} %pad_clamp_fusion.1), kind=kCustom, calls=%fused_computation.1 | custom fusion | bytes 9437760 | tf_op jit(solution)/shard_map/gather | solution.py:36
  84.9 101.2 %while.24 = (s32[]{:T(128)}, f32[256,12,128]{2,1,0:T(8,128)}, s32[9,16]{1,0:T(8,128)S(1)}, bf16[9,16,128,128]{3,2,1,0:T(8,128)(2,1)}, s32[9,16]{1,0:T(8,128)S(1)...) while((s32[]{:T(128)}, f32[256,12,128]{2,1,0:T(8,128)}, s32[9,16]{1,0:T(8,128)S(1)}, ...), condition=%wide.region_2.3_spmd.clone, body=%wide.region_1.2_spmd.clone.sunk | while | flops 261358528 | bytes 17302000 | solution.py:78
  102.1 4.8 bitcast_add_fusion.4
  113.4 4.8 bitcast_add_fusion.4
  124.8 4.8 bitcast_add_fusion.4
  136.1 4.8 bitcast_add_fusion.4
  181.4 4.8 bitcast_add_fusion.4
  195.4 180.7 %while.25 = (s32[]{:T(128)}, f32[256,48,128]{2,1,0:T(8,128)}, bf16[9,16,128,128]{3,2,1,0:T(8,128)(2,1)}, s32[9,16]{1,0:T(8,128)S(1)}, bf16[9,16,128,128]{3,2,1,0...) while((s32[]{:T(128)}, f32[256,48,128]{2,1,0:T(8,128)}, ...), condition=%wide.region_4.5_spmd.clone, body=%wide.region_3.4_spmd.clone.sunk | while | flops 637535936 | bytes 40108668 | solution.py:104
  204.0 7.2 %bitcast_add_fusion.5 = f32[256,48,128]{2,1,0:T(8,128)} fusion(f32[256,48,128]{2,1,0:T(8,128)} %get-tuple-element.344, pred[]{:T(512)S(6)} %compare.100, f32[256,16,128]{2,1,0:T(8,128)} %copy.50, s32[16]{0:T(128)S(1)} %get-tuple-element.308), kind=kOutput, calls=%fused_computation.22.clone.1 | convolution fusion | flops 305136384 | bytes 14680129 | tf_op jit(solution)/shard_map/while/body/eval_jaxpr/tgb,gr->trb/dot_general | solution.py:101
  222.4 9.0 %bitcast_add_fusion.5 = f32[256,48,128]{2,1,0:T(8,128)} fusion(f32[256,48,128]{2,1,0:T(8,128)} %get-tuple-element.344, pred[]{:T(512)S(6)} %compare.100, f32[256,16,128]{2,1,0:T(8,128)} %copy.50, s32[16]{0:T(128)S(1)} %get-tuple-element.308), kind=kOutput, calls=%fused_computation.22.clone.1 | convolution fusion | flops 305136384 | bytes 14680129 | tf_op jit(solution)/shard_map/while/body/eval_jaxpr/tgb,gr->trb/dot_general | solution.py:101
  242.7 9.0 %bitcast_add_fusion.5 = f32[256,48,128]{2,1,0:T(8,128)} fusion(f32[256,48,128]{2,1,0:T(8,128)} %get-tuple-element.344, pred[]{:T(512)S(6)} %compare.100, f32[256,16,128]{2,1,0:T(8,128)} %copy.50, s32[16]{0:T(128)S(1)} %get-tuple-element.308), kind=kOutput, calls=%fused_computation.22.clone.1 | convolution fusion | flops 305136384 | bytes 14680129 | tf_op jit(solution)/shard_map/while/body/eval_jaxpr/tgb,gr->trb/dot_general | solution.py:101
  263.0 9.0 %bitcast_add_fusion.5 = f32[256,48,128]{2,1,0:T(8,128)} fusion(f32[256,48,128]{2,1,0:T(8,128)} %get-tuple-element.344, pred[]{:T(512)S(6)} %compare.100, f32[256,16,128]{2,1,0:T(8,128)} %copy.50, s32[16]{0:T(128)S(1)} %get-tuple-element.308), kind=kOutput, calls=%fused_computation.22.clone.1 | convolution fusion | flops 305136384 | bytes 14680129 | tf_op jit(solution)/shard_map/while/body/eval_jaxpr/tgb,gr->trb/dot_general | solution.py:101
  283.2 9.0 %bitcast_add_fusion.5 = f32[256,48,128]{2,1,0:T(8,128)} fusion(f32[256,48,128]{2,1,0:T(8,128)} %get-tuple-element.344, pred[]{:T(512)S(6)} %compare.100, f32[256,16,128]{2,1,0:T(8,128)} %copy.50, s32[16]{0:T(128)S(1)} %get-tuple-element.308), kind=kOutput, calls=%fused_computation.22.clone.1 | convolution fusion | flops 305136384 | bytes 14680129 | tf_op jit(solution)/shard_map/while/body/eval_jaxpr/tgb,gr->trb/dot_general | solution.py:101
  303.5 9.0 %bitcast_add_fusion.5 = f32[256,48,128]{2,1,0:T(8,128)} fusion(f32[256,48,128]{2,1,0:T(8,128)} %get-tuple-element.344, pred[]{:T(512)S(6)} %compare.100, f32[256,16,128]{2,1,0:T(8,128)} %copy.50, s32[16]{0:T(128)S(1)} %get-tuple-element.308), kind=kOutput, calls=%fused_computation.22.clone.1 | convolution fusion | flops 305136384 | bytes 14680129 | tf_op jit(solution)/shard_map/while/body/eval_jaxpr/tgb,gr->trb/dot_general | solution.py:101
  323.8 9.0 %bitcast_add_fusion.5 = f32[256,48,128]{2,1,0:T(8,128)} fusion(f32[256,48,128]{2,1,0:T(8,128)} %get-tuple-element.344, pred[]{:T(512)S(6)} %compare.100, f32[256,16,128]{2,1,0:T(8,128)} %copy.50, s32[16]{0:T(128)S(1)} %get-tuple-element.308), kind=kOutput, calls=%fused_computation.22.clone.1 | convolution fusion | flops 305136384 | bytes 14680129 | tf_op jit(solution)/shard_map/while/body/eval_jaxpr/tgb,gr->trb/dot_general | solution.py:101
  344.1 9.0 %bitcast_add_fusion.5 = f32[256,48,128]{2,1,0:T(8,128)} fusion(f32[256,48,128]{2,1,0:T(8,128)} %get-tuple-element.344, pred[]{:T(512)S(6)} %compare.100, f32[256,16,128]{2,1,0:T(8,128)} %copy.50, s32[16]{0:T(128)S(1)} %get-tuple-element.308), kind=kOutput, calls=%fused_computation.22.clone.1 | convolution fusion | flops 305136384 | bytes 14680129 | tf_op jit(solution)/shard_map/while/body/eval_jaxpr/tgb,gr->trb/dot_general | solution.py:101
  364.4 9.0 %bitcast_add_fusion.5 = f32[256,48,128]{2,1,0:T(8,128)} fusion(f32[256,48,128]{2,1,0:T(8,128)} %get-tuple-element.344, pred[]{:T(512)S(6)} %compare.100, f32[256,16,128]{2,1,0:T(8,128)} %copy.50, s32[16]{0:T(128)S(1)} %get-tuple-element.308), kind=kOutput, calls=%fused_computation.22.clone.1 | convolution fusion | flops 305136384 | bytes 14680129 | tf_op jit(solution)/shard_map/while/body/eval_jaxpr/tgb,gr->trb/dot_general | solution.py:101
  383.8 12.6 %gather_fusion.2 = bf16[288,128,128]{2,1,0:T(8,128)(2,1)} fusion(bf16[144,128,128]{2,1,0:T(8,128)(2,1)} %bitcast.145, s32[1024]{0:T(1024)S(1)} %pad_clamp_fusion), kind=kCustom, calls=%fused_computation.2 | custom fusion | bytes 18875520 | tf_op jit(solution)/shard_map/gather | solution.py:121
  396.4 9.3 %select_convert_fusion = bf16[288,128,128]{2,1,0:T(8,128)(2,1)} fusion(bf16[288,128,128]{2,1,0:T(8,128)(2,1)} %gather_fusion.2, pred[288]{0:T(512)(128)(4,1)S(1)} %broadcast_compare_fusion.1), kind=kLoop, calls=%fused_computation.47 | loop fusion | flops 4718592 | bytes 18874656 | tf_op jit(solution)/shard_map/convert_element_type | solution.py:123
  408.0 53.7 %reduce-scatter.7.cloned.1.call-done = bf16[384,256]{1,0:T(8,128)(2,1)} async-done(((bf16[6144,256]{1,0:T(8,128)(2,1)}), bf16[384,256]{1,0:T(8,128)(2,1)}) %reduce-scatter.7.cloned.1.call-update) | async-done | bytes 196624
  463.5 73.3 %reduce-scatter.5.cloned.1.call-done = bf16[18,128,128]{2,1,0:T(8,128)(2,1)} async-done(((bf16[288,128,128]{2,1,0:T(8,128)(2,1)}), bf16[18,128,128]{2,1,0:T(8,128)(2,1)}) %reduce-scatter.5.cloned.1.call-update) | async-done | bytes 589840 | tf_op jit(solution)/shard_map/reduce_scatter | solution.py:122
  (183 shorter events, 221.0 us)
Async XLA Ops:
  7.2 66.5 %all-gather.2.cloned.1.call-start = ((), (), s32[]{:S(2)}) async-start(), calls=%async_computation.2 | async-start | bytes 10027008 | tf_op jit(solution)/shard_map/all_gather | solution.py:56
  7.9 453.8 %reduce-scatter.7.cloned.1.call-start = ((), (), s32[]{:S(2)}) async-start(), calls=%async_computation.4 | async-start | bytes 3342336
  197.1 1.0 copy-start
  211.2 1.2 copy-start.1
  215.5 1.0 copy-start
  231.4 1.2 copy-start.1
  235.8 1.0 copy-start
  251.7 1.2 copy-start.1
  256.1 1.0 copy-start
  272.0 1.2 copy-start.1
  276.3 1.0 copy-start
  292.3 1.2 copy-start.1
  296.6 1.0 copy-start
  312.6 1.2 copy-start.1
  316.9 1.0 copy-start
  332.9 1.2 copy-start.1
  337.2 1.0 copy-start
  353.1 1.2 copy-start.1
  357.5 1.0 copy-start
  373.4 1.2 copy-start.1
  382.6 154.2 %reduce-scatter.5.cloned.1.call-start = ((), (), s32[]{:S(2)}) async-start(), calls=%async_computation.3 | async-start | bytes 10027008 | tf_op jit(solution)/shard_map/reduce_scatter | solution.py:122
  405.7 1.2 copy-start.2
Sparse Core Ops, SparseCore 0:
  9.8 63.7 all-gather.1
  382.7 78.9 reduce-scatter.6
  464.3 72.4 reduce-scatter.4
where the time goes:
time: 548 us; the launch traced here: 545 us
  matrix products  211 us (39%)
  waiting for transfers between devices  151 us (28%)
  local copies, waits for them, and re-layouts  118 us (22%)
  other arithmetic  32.6 us (6%)
  blocking collectives  16.4 us (3%)
  between operations  15.2 us (3%)
    dot_general x9, matrix products, backward_group(): jnp.einsum('tgb,gr->trb', contrib, rows_place, precision=lax.Precision.HI...  79.4 us
    reduce_scatter x1, waiting for transfers between devices, per_device(): lax.psum_scatter(jnp.where((position >= 0)[:, None, None], picked, 0.0).a...  73.3 us
    unnamed x4, waiting for transfers between devices  54.4 us
    dot_general x9, matrix products, forward_group(): jnp.einsum('tgc,gk->tkc', product, cols_hot, precision=lax.Precision.HIGH...  42.3 us
    transpose x9, local copies, waits for them, and re-layouts, backward_group(): jnp.einsum('tgc,gbc->tgb', grad_piece, block_piece, preferred_element_typ...  27.9 us
    transpose x9, local copies, waits for them, and re-layouts, forward_group(): jnp.einsum('tgb,gbc->tgc', x_rows, block_piece, preferred_element_type=jn...  27.9 us
    dot_general x9, matrix products, forward_group(): jnp.einsum('tgb,gbc->tgc', x_rows, block_piece, preferred_element_type=jn...  25.5 us
    dot_general x9, matrix products, backward_group(): jnp.einsum('tgc,gbc->tgb', grad_piece, block_piece, preferred_element_typ...  25.1 us
  transfers between devices with their start and end apart: 3, of which 3 were waited for; matrix products, arithmetic and copies ran while one was open for 9% of the time, Pallas kernels for 0%

commit v1 on v0

--- a/solution.py
+++ b/solution.py
@@ -6,6 +6,22 @@
 
 GELU_C = 0.7978845608028654
 GELU_A = 0.044715
+
+
+def ring_gather(x, axis, dim):
+    ways, here, step = (lax.axis_size(axis), lax.axis_index(axis), x.shape[dim])
+    shape = [n * ways if d == dim else n for d, n in enumerate(x.shape)]
+    full = lax.dynamic_update_slice_in_dim(jnp.zeros(shape, x.dtype), x, here * step, axis=dim)
+    going_up = going_down = x
+    for far in range(1, ways // 2 + 1):
+        going_up = lax.ppermute(going_up, axis, [(d, (d + 1) % ways) for d in range(ways)])
+        full = lax.dynamic_update_slice_in_dim(full, going_up, (here - far) % ways * step, axis=dim)
+        if 2 * far < ways:
+            going_down = lax.ppermute(going_down, axis, [(d, (d - 1) % ways) for d in range(ways)])
+            full = lax.dynamic_update_slice_in_dim(
+                full, going_down, (here + far) % ways * step, axis=dim
+            )
+    return full
 
 
 def gelu_value(values):
@@ -53,7 +69,7 @@
     group_count = lax.axis_size("dp")
     x_blocks = inputs.reshape(tok_rows, row_blocks, block_size)
     gathered = (
-        lax.all_gather(w_blocks, "dp", axis=1, tiled=True),
+        ring_gather(w_blocks, "dp", 1),
         lax.all_gather(block_ids, "dp", axis=1, tiled=True),
         lax.all_gather(counts, "dp", axis=1, tiled=True),
     )

time: 548 us -> 584 us (1.066)
  starting transfers between devices: 0.12 us -> 23.5 us
  local copies, waits for them, and re-layouts: 118 us -> 140 us
  waiting for transfers between devices: 151 us -> 143 us
    all_gather x1 -> x0, waiting for transfers between devices: 23.5 us -> none  [per_device(): lax.all_gather(w_blocks, 'dp', axis=1, tiled=True)]
    ppermute x0 -> x15, starting transfers between devices: none -> 23.5 us  [the longest x7 23.4 us: ring_gather(): lax.ppermute(going_down, axis, [(d, (d - 1) % ways) for d in range(ways)])]
    dynamic_update_slice x0 -> x16, local copies, waits for them, and re-layouts: none -> 21.5 us  [the longest x8 11.4 us: ring_gather(): lax.dynamic_update_slice_in_dim(full, going_up, (here - far) % ways * ste...]
    ppermute x0 -> x15, waiting for transfers between devices: none -> 17.6 us  [the longest x7 10.9 us: ring_gather(): lax.ppermute(going_down, axis, [(d, (d - 1) % ways) for d in range(ways)])]
    squeeze x0 -> x1, local copies, waits for them, and re-layouts: none -> 6.02 us  [select_live(): blocks = gathered[0][0]]
    unnamed x4 -> x3, waiting for transfers between devices: 54.4 us -> 52.6 us
    unnamed x13 -> x21, local copies, waits for them, and re-layouts: 17.7 us -> 17.6 us
  transfers between devices with their start and end apart: 3 -> 17, of which waited for: 3 -> 10; matrix products, arithmetic and copies ran while one was open for 9% -> 13% of each run, Pallas kernels for 0% -> 0%
where the time goes in v1:
time: 584 us; the launch traced here: 581 us
  matrix products  212 us (36%)
  waiting for transfers between devices  143 us (24%)
  local copies, waits for them, and re-layouts  140 us (24%)
  other arithmetic  32.5 us (6%)
  starting transfers between devices  23.5 us (4%)
  between operations  15.8 us (3%)
  blocking collectives  13.4 us (2%)
    dot_general x9, matrix products, backward_group(): jnp.einsum('tgb,gr->trb', contrib, rows_place, precision=lax.Precision.HI...  80.1 us
    reduce_scatter x1, waiting for transfers between devices, per_device(): lax.psum_scatter(jnp.where((position >= 0)[:, None, None], picked, 0.0).a...  73.1 us
    unnamed x3, waiting for transfers between devices  52.6 us
    dot_general x9, matrix products, forward_group(): jnp.einsum('tgc,gk->tkc', product, cols_hot, precision=lax.Precision.HIGH...  42.3 us
    transpose x9, local copies, waits for them, and re-layouts, forward_group(): jnp.einsum('tgb,gbc->tgc', x_rows, block_piece, preferred_element_type=jn...  27.9 us
    transpose x9, local copies, waits for them, and re-layouts, backward_group(): jnp.einsum('tgc,gbc->tgb', grad_piece, block_piece, preferred_element_typ...  27.9 us
    dot_general x9, matrix products, forward_group(): jnp.einsum('tgb,gbc->tgc', x_rows, block_piece, preferred_element_type=jn...  25.5 us
    dot_general x9, matrix products, backward_group(): jnp.einsum('tgc,gbc->tgb', grad_piece, block_piece, preferred_element_typ...  25.1 us
  transfers between devices with their start and end apart: 17, of which 10 were waited for; matrix products, arithmetic and copies ran while one was open for 13% of the time, Pallas kernels for 0%

profile of v1, /device:TPU:6, one launch (start us, length us, event | category | flops | bytes accessed | tf_op | source)
XLA Modules:
  0.0 581.2 jit_solution(7284132430312332750)
XLA Ops:
  7.2 5.3 collective-permute-start.1
  16.6 13.4 %all-reduce.2 = (s32[288]{0:T(512)S(1)}, s32[16]{0:T(128)S(1)}) all-reduce(s32[288]{0:T(512)S(1)} %bitcast_dynamic-update-slice_fusion.17, s32[16]{0:T(128)S(1)} %bitcast_dynamic-update-slice_fusion.16), channel_id=1, replica_groups=mesh['dp'=16,'tensor'=16] {'dp'}, use_global_device_ids=true, to_apply=%add | all-reduce | flops 304 | bytes 2432 | tf_op jit(solution)/shard_map/squeeze | solution.py:42
  35.4 5.6 fusion.44
  49.4 6.0 %squeeze.55 = bf16[288,128,128]{2,1,0:T(8,128)(2,1)} broadcast(bf16[]{:T(256)} %constant.175.clone.1), dimensions={} | broadcast | bytes 9437186 | tf_op jit(solution)/shard_map/squeeze | solution.py:41
  115.3 11.2 %gather_fusion.1 = bf16[144,128,128]{2,1,0:T(8,128)(2,1)} fusion(bf16[288,128,128]{2,1,0:T(8,128)(2,1)} %bitcast_dynamic-update-slice_fusion, s32[1024]{0:T(1024)S(1)} %pad_clamp_fusion.1), kind=kCustom, calls=%fused_computation.1 | custom fusion | bytes 9437760 | tf_op jit(solution)/shard_map/gather | solution.py:52
  126.5 101.2 %while.24 = (s32[]{:T(128)}, f32[256,12,128]{2,1,0:T(8,128)}, s32[9,16]{1,0:T(8,128)S(1)}, bf16[9,16,128,128]{3,2,1,0:T(8,128)(2,1)}, s32[9,16]{1,0:T(8,128)S(1)...) while((s32[]{:T(128)}, f32[256,12,128]{2,1,0:T(8,128)}, s32[9,16]{1,0:T(8,128)S(1)}, ...), condition=%wide.region_2.3_spmd.clone, body=%wide.region_1.2_spmd.clone.sunk | while | flops 261358528 | bytes 17302000 | solution.py:94
  143.8 4.8 bitcast_add_fusion.4
  155.1 4.8 bitcast_add_fusion.4
  166.4 4.8 bitcast_add_fusion.4
  189.0 4.8 bitcast_add_fusion.4
  237.0 175.9 %while.25 = (s32[]{:T(128)}, f32[256,48,128]{2,1,0:T(8,128)}, bf16[9,16,128,128]{3,2,1,0:T(8,128)(2,1)}, s32[9,16]{1,0:T(8,128)S(1)}, bf16[9,16,128,128]{3,2,1,0...) while((s32[]{:T(128)}, f32[256,48,128]{2,1,0:T(8,128)}, ...), condition=%wide.region_4.5_spmd.clone, body=%wide.region_3.4_spmd.clone.sunk | while | flops 637535936 | bytes 40108668 | solution.py:120
  245.6 7.3 %bitcast_add_fusion.5 = f32[256,48,128]{2,1,0:T(8,128)} fusion(f32[256,48,128]{2,1,0:T(8,128)} %get-tuple-element.352, pred[]{:T(512)S(6)} %compare.115, f32[256,16,128]{2,1,0:T(8,128)} %copy.49, s32[16]{0:T(128)S(1)} %get-tuple-element.316), kind=kOutput, calls=%fused_computation.22.clone.1 | convolution fusion | flops 305136384 | bytes 14680129 | tf_op jit(solution)/shard_map/while/body/eval_jaxpr/tgb,gr->trb/dot_general | solution.py:117
  263.5 9.1 %bitcast_add_fusion.5 = f32[256,48,128]{2,1,0:T(8,128)} fusion(f32[256,48,128]{2,1,0:T(8,128)} %get-tuple-element.352, pred[]{:T(512)S(6)} %compare.115, f32[256,16,128]{2,1,0:T(8,128)} %copy.49, s32[16]{0:T(128)S(1)} %get-tuple-element.316), kind=kOutput, calls=%fused_computation.22.clone.1 | convolution fusion | flops 305136384 | bytes 14680129 | tf_op jit(solution)/shard_map/while/body/eval_jaxpr/tgb,gr->trb/dot_general | solution.py:117
  283.3 9.1 %bitcast_add_fusion.5 = f32[256,48,128]{2,1,0:T(8,128)} fusion(f32[256,48,128]{2,1,0:T(8,128)} %get-tuple-element.352, pred[]{:T(512)S(6)} %compare.115, f32[256,16,128]{2,1,0:T(8,128)} %copy.49, s32[16]{0:T(128)S(1)} %get-tuple-element.316), kind=kOutput, calls=%fused_computation.22.clone.1 | convolution fusion | flops 305136384 | bytes 14680129 | tf_op jit(solution)/shard_map/while/body/eval_jaxpr/tgb,gr->trb/dot_general | solution.py:117
  303.0 9.1 %bitcast_add_fusion.5 = f32[256,48,128]{2,1,0:T(8,128)} fusion(f32[256,48,128]{2,1,0:T(8,128)} %get-tuple-element.352, pred[]{:T(512)S(6)} %compare.115, f32[256,16,128]{2,1,0:T(8,128)} %copy.49, s32[16]{0:T(128)S(1)} %get-tuple-element.316), kind=kOutput, calls=%fused_computation.22.clone.1 | convolution fusion | flops 305136384 | bytes 14680129 | tf_op jit(solution)/shard_map/while/body/eval_jaxpr/tgb,gr->trb/dot_general | solution.py:117
  322.8 9.1 %bitcast_add_fusion.5 = f32[256,48,128]{2,1,0:T(8,128)} fusion(f32[256,48,128]{2,1,0:T(8,128)} %get-tuple-element.352, pred[]{:T(512)S(6)} %compare.115, f32[256,16,128]{2,1,0:T(8,128)} %copy.49, s32[16]{0:T(128)S(1)} %get-tuple-element.316), kind=kOutput, calls=%fused_computation.22.clone.1 | convolution fusion | flops 305136384 | bytes 14680129 | tf_op jit(solution)/shard_map/while/body/eval_jaxpr/tgb,gr->trb/dot_general | solution.py:117
  342.5 9.1 %bitcast_add_fusion.5 = f32[256,48,128]{2,1,0:T(8,128)} fusion(f32[256,48,128]{2,1,0:T(8,128)} %get-tuple-element.352, pred[]{:T(512)S(6)} %compare.115, f32[256,16,128]{2,1,0:T(8,128)} %copy.49, s32[16]{0:T(128)S(1)} %get-tuple-element.316), kind=kOutput, calls=%fused_computation.22.clone.1 | convolution fusion | flops 305136384 | bytes 14680129 | tf_op jit(solution)/shard_map/while/body/eval_jaxpr/tgb,gr->trb/dot_general | solution.py:117
  362.3 9.1 %bitcast_add_fusion.5 = f32[256,48,128]{2,1,0:T(8,128)} fusion(f32[256,48,128]{2,1,0:T(8,128)} %get-tuple-element.352, pred[]{:T(512)S(6)} %compare.115, f32[256,16,128]{2,1,0:T(8,128)} %copy.49, s32[16]{0:T(128)S(1)} %get-tuple-element.316), kind=kOutput, calls=%fused_computation.22.clone.1 | convolution fusion | flops 305136384 | bytes 14680129 | tf_op jit(solution)/shard_map/while/body/eval_jaxpr/tgb,gr->trb/dot_general | solution.py:117
  382.1 9.1 %bitcast_add_fusion.5 = f32[256,48,128]{2,1,0:T(8,128)} fusion(f32[256,48,128]{2,1,0:T(8,128)} %get-tuple-element.352, pred[]{:T(512)S(6)} %compare.115, f32[256,16,128]{2,1,0:T(8,128)} %copy.49, s32[16]{0:T(128)S(1)} %get-tuple-element.316), kind=kOutput, calls=%fused_computation.22.clone.1 | convolution fusion | flops 305136384 | bytes 14680129 | tf_op jit(solution)/shard_map/while/body/eval_jaxpr/tgb,gr->trb/dot_general | solution.py:117
  401.8 9.1 %bitcast_add_fusion.5 = f32[256,48,128]{2,1,0:T(8,128)} fusion(f32[256,48,128]{2,1,0:T(8,128)} %get-tuple-element.352, pred[]{:T(512)S(6)} %compare.115, f32[256,16,128]{2,1,0:T(8,128)} %copy.49, s32[16]{0:T(128)S(1)} %get-tuple-element.316), kind=kOutput, calls=%fused_computation.22.clone.1 | convolution fusion | flops 305136384 | bytes 14680129 | tf_op jit(solution)/shard_map/while/body/eval_jaxpr/tgb,gr->trb/dot_general | solution.py:117
  420.7 12.6 %gather_fusion.2 = bf16[288,128,128]{2,1,0:T(8,128)(2,1)} fusion(bf16[144,128,128]{2,1,0:T(8,128)(2,1)} %bitcast.175, s32[1024]{0:T(1024)S(1)} %pad_clamp_fusion), kind=kCustom, calls=%fused_computation.2 | custom fusion | bytes 18875520 | tf_op jit(solution)/shard_map/gather | solution.py:137
  433.3 9.3 %select_convert_fusion = bf16[288,128,128]{2,1,0:T(8,128)(2,1)} fusion(bf16[288,128,128]{2,1,0:T(8,128)(2,1)} %gather_fusion.2, pred[288]{0:T(512)(128)(4,1)S(1)} %broadcast_compare_fusion.1), kind=kLoop, calls=%fused_computation.47 | loop fusion | flops 4718592 | bytes 18874656 | tf_op jit(solution)/shard_map/convert_element_type | solution.py:139
  444.9 52.6 %reduce-scatter.7.cloned.1.call-done = bf16[384,256]{1,0:T(8,128)(2,1)} async-done(((bf16[6144,256]{1,0:T(8,128)(2,1)}), bf16[384,256]{1,0:T(8,128)(2,1)}) %reduce-scatter.7.cloned.1.call-update) | async-done | bytes 196624
  499.2 73.1 %reduce-scatter.5.cloned.1.call-done = bf16[18,128,128]{2,1,0:T(8,128)(2,1)} async-done(((bf16[288,128,128]{2,1,0:T(8,128)(2,1)}), bf16[18,128,128]{2,1,0:T(8,128)(2,1)}) %reduce-scatter.5.cloned.1.call-update) | async-done | bytes 589840 | tf_op jit(solution)/shard_map/reduce_scatter | solution.py:138
  (231 shorter events, 276.5 us)
Async XLA Ops:
  7.2 490.3 %reduce-scatter.7.cloned.1.call-start = ((), (), s32[]{:S(2)}) async-start(), calls=%async_computation.3 | async-start | bytes 3342336
  7.2 22.8 %collective-permute-start = (bf16[1,18,128,128]{3,2,1,0:T(8,128)(2,1)}, bf16[1,18,128,128]{3,2,1,0:T(8,128)(2,1)S(1)}, u32[]{:S(2)}, u32[]{:S(2)}) collective-permute-start(bf16[1,18,128,128]{3,2,1,0:T(8,128)(2,1)} %param.11), channel_id=1, source_target_pairs={{0,16},{16,32},{32,48},{48,64},{64,80},{80,96},{96,112},{112,128},... | collective-permute-start | bytes 1769480 | tf_op jit(solution)/shard_map/ppermute | solution.py:17
  7.2 37.6 %collective-permute-start.1 = (bf16[1,18,128,128]{3,2,1,0:T(8,128)(2,1)}, bf16[1,18,128,128]{3,2,1,0:T(8,128)(2,1)S(1)}, u32[]{:S(2)}, u32[]{:S(2)}) collective-permute-start(bf16[1,18,128,128]{3,2,1,0:T(8,128)(2,1)} %param.11), channel_id=1, source_target_pairs={{0,240},{16,0},{32,16},{48,32},{64,48},{80,64},{96,80},{112,96},{1... | collective-permute-start | bytes 1769480 | tf_op jit(solution)/shard_map/ppermute | solution.py:20
  30.0 25.5 %copy-start.5 = (bf16[1,18,128,128]{3,2,1,0:T(8,128)(2,1)}, bf16[1,18,128,128]{3,2,1,0:T(8,128)(2,1)S(1)}, u32[]{:S(2)}) copy-start(bf16[1,18,128,128]{3,2,1,0:T(8,128)(2,1)S(1)} %collective-permute-done) | copy-start | bytes 1769476
  30.0 19.3 %collective-permute-start.2 = (bf16[1,18,128,128]{3,2,1,0:T(8,128)(2,1)S(1)}, bf16[1,18,128,128]{3,2,1,0:T(8,128)(2,1)S(1)}, u32[]{:S(2)}, u32[]{:S(2)}) collective-permute-start(bf16[1,18,128,128]{3,2,1,0:T(8,128)(2,1)S(1)} %collective-permute-done), channel_id=1, source_target_pairs={{0,16},{16,32},{32,48},{48,64},{64,80},{80,96},{96,112},{112,128},... | collective-permute-start | bytes 1769480 | tf_op jit(solution)/shard_map/ppermute | solution.py:17
  44.9 10.6 %copy-start.4 = (bf16[1,18,128,128]{3,2,1,0:T(8,128)(2,1)}, bf16[1,18,128,128]{3,2,1,0:T(8,128)(2,1)S(1)}, u32[]{:S(2)}) copy-start(bf16[1,18,128,128]{3,2,1,0:T(8,128)(2,1)S(1)} %collective-permute-done.1) | copy-start | bytes 1769476
  44.9 11.4 %collective-permute-start.3 = (bf16[1,18,128,128]{3,2,1,0:T(8,128)(2,1)S(1)}, bf16[1,18,128,128]{3,2,1,0:T(8,128)(2,1)}, u32[]{:S(2)}, u32[]{:S(2)}) collective-permute-start(bf16[1,18,128,128]{3,2,1,0:T(8,128)(2,1)S(1)} %collective-permute-done.1), channel_id=1, source_target_pairs={{0,240},{16,0},{32,16},{48,32},{64,48},{80,64},{96,80},{112,96},{1... | collective-permute-start | bytes 1769480 | tf_op jit(solution)/shard_map/ppermute | solution.py:20
  49.4 10.6 %collective-permute-start.4 = (bf16[1,18,128,128]{3,2,1,0:T(8,128)(2,1)S(1)}, bf16[1,18,128,128]{3,2,1,0:T(8,128)(2,1)}, u32[]{:S(2)}, u32[]{:S(2)}) collective-permute-start(bf16[1,18,128,128]{3,2,1,0:T(8,128)(2,1)S(1)} %collective-permute-done.2), channel_id=1, source_target_pairs={{0,16},{16,32},{32,48},{48,64},{64,80},{80,96},{96,112},{112,128},... | collective-permute-start | bytes 1769480 | tf_op jit(solution)/shard_map/ppermute | solution.py:17
  56.3 10.9 %collective-permute-start.5 = (bf16[1,18,128,128]{3,2,1,0:T(8,128)(2,1)}, bf16[1,18,128,128]{3,2,1,0:T(8,128)(2,1)}, u32[]{:S(2)}, u32[]{:S(2)}) collective-permute-start(bf16[1,18,128,128]{3,2,1,0:T(8,128)(2,1)} %collective-permute-done.3), channel_id=1, source_target_pairs={{0,240},{16,0},{32,16},{48,32},{64,48},{80,64},{96,80},{112,96},{1... | collective-permute-start | bytes 1769480 | tf_op jit(solution)/shard_map/ppermute | solution.py:20
  60.0 12.1 %collective-permute-start.6 = (bf16[1,18,128,128]{3,2,1,0:T(8,128)(2,1)}, bf16[1,18,128,128]{3,2,1,0:T(8,128)(2,1)}, u32[]{:S(2)}, u32[]{:S(2)}) collective-permute-start(bf16[1,18,128,128]{3,2,1,0:T(8,128)(2,1)} %collective-permute-done.4), channel_id=1, source_target_pairs={{0,16},{16,32},{32,48},{48,64},{64,80},{80,96},{96,112},{112,128},... | collective-permute-start | bytes 1769480 | tf_op jit(solution)/shard_map/ppermute | solution.py:17
  67.2 10.7 %collective-permute-start.7 = (bf16[1,18,128,128]{3,2,1,0:T(8,128)(2,1)}, bf16[1,18,128,128]{3,2,1,0:T(8,128)(2,1)S(1)}, u32[]{:S(2)}, u32[]{:S(2)}) collective-permute-start(bf16[1,18,128,128]{3,2,1,0:T(8,128)(2,1)} %collective-permute-done.5), channel_id=1, source_target_pairs={{0,240},{16,0},{32,16},{48,32},{64,48},{80,64},{96,80},{112,96},{1... | collective-permute-start | bytes 1769480 | tf_op jit(solution)/shard_map/ppermute | solution.py:20
  72.1 10.7 %collective-permute-start.8 = (bf16[1,18,128,128]{3,2,1,0:T(8,128)(2,1)}, bf16[1,18,128,128]{3,2,1,0:T(8,128)(2,1)S(1)}, u32[]{:S(2)}, u32[]{:S(2)}) collective-permute-start(bf16[1,18,128,128]{3,2,1,0:T(8,128)(2,1)} %collective-permute-done.6), channel_id=1, source_target_pairs={{0,16},{16,32},{32,48},{48,64},{64,80},{80,96},{96,112},{112,128},... | collective-permute-start | bytes 1769480 | tf_op jit(solution)/shard_map/ppermute | solution.py:17
  77.9 10.4 %collective-permute-start.9 = (bf16[1,18,128,128]{3,2,1,0:T(8,128)(2,1)S(1)}, bf16[1,18,128,128]{3,2,1,0:T(8,128)(2,1)S(1)}, u32[]{:S(2)}, u32[]{:S(2)}) collective-permute-start(bf16[1,18,128,128]{3,2,1,0:T(8,128)(2,1)S(1)} %collective-permute-done.7), channel_id=1, source_target_pairs={{0,240},{16,0},{32,16},{48,32},{64,48},{80,64},{96,80},{112,96},{1... | collective-permute-start | bytes 1769480 | tf_op jit(solution)/shard_map/ppermute | solution.py:20
  82.8 10.5 %collective-permute-start.10 = (bf16[1,18,128,128]{3,2,1,0:T(8,128)(2,1)S(1)}, bf16[1,18,128,128]{3,2,1,0:T(8,128)(2,1)S(1)}, u32[]{:S(2)}, u32[]{:S(2)}) collective-permute-start(bf16[1,18,128,128]{3,2,1,0:T(8,128)(2,1)S(1)} %collective-permute-done.8), channel_id=1, source_target_pairs={{0,16},{16,32},{32,48},{48,64},{64,80},{80,96},{96,112},{112,128},... | collective-permute-start | bytes 1769480 | tf_op jit(solution)/shard_map/ppermute | solution.py:17
  88.3 10.5 %collective-permute-start.11 = (bf16[1,18,128,128]{3,2,1,0:T(8,128)(2,1)S(1)}, bf16[1,18,128,128]{3,2,1,0:T(8,128)(2,1)S(1)}, u32[]{:S(2)}, u32[]{:S(2)}) collective-permute-start(bf16[1,18,128,128]{3,2,1,0:T(8,128)(2,1)S(1)} %collective-permute-done.9), channel_id=1, source_target_pairs={{0,240},{16,0},{32,16},{48,32},{64,48},{80,64},{96,80},{112,96},{1... | collective-permute-start | bytes 1769480 | tf_op jit(solution)/shard_map/ppermute | solution.py:20
  93.4 10.5 %collective-permute-start.12 = (bf16[1,18,128,128]{3,2,1,0:T(8,128)(2,1)S(1)}, bf16[1,18,128,128]{3,2,1,0:T(8,128)(2,1)S(1)}, u32[]{:S(2)}, u32[]{:S(2)}) collective-permute-start(bf16[1,18,128,128]{3,2,1,0:T(8,128)(2,1)S(1)} %collective-permute-done.10), channel_id=1, source_target_pairs={{0,16},{16,32},{32,48},{48,64},{64,80},{80,96},{96,112},{112,128},... | collective-permute-start | bytes 1769480 | tf_op jit(solution)/shard_map/ppermute | solution.py:17
  98.8 10.5 %collective-permute-start.13 = (bf16[1,18,128,128]{3,2,1,0:T(8,128)(2,1)S(1)}, bf16[1,18,128,128]{3,2,1,0:T(8,128)(2,1)S(1)}, u32[]{:S(2)}, u32[]{:S(2)}) collective-permute-start(bf16[1,18,128,128]{3,2,1,0:T(8,128)(2,1)S(1)} %collective-permute-done.11), channel_id=1, source_target_pairs={{0,240},{16,0},{32,16},{48,32},{64,48},{80,64},{96,80},{112,96},{1... | collective-permute-start | bytes 1769480 | tf_op jit(solution)/shard_map/ppermute | solution.py:20
  103.9 10.5 %collective-permute-start.14 = (bf16[1,18,128,128]{3,2,1,0:T(8,128)(2,1)S(1)}, bf16[1,18,128,128]{3,2,1,0:T(8,128)(2,1)S(1)}, u32[]{:S(2)}, u32[]{:S(2)}) collective-permute-start(bf16[1,18,128,128]{3,2,1,0:T(8,128)(2,1)S(1)} %collective-permute-done.12), channel_id=1, source_target_pairs={{0,16},{16,32},{32,48},{48,64},{64,80},{80,96},{96,112},{112,128},... | collective-permute-start | bytes 1769480 | tf_op jit(solution)/shard_map/ppermute | solution.py:17
  263.5 9.7 %copy-start.1 = (bf16[256,16,128]{2,1,0:T(8,128)(2,1)S(1)}, bf16[256,16,128]{2,1,0:T(8,128)(2,1)}, u32[]{:S(2)}) copy-start(bf16[256,16,128]{2,1,0:T(8,128)(2,1)} %copy-done) | copy-start | bytes 3145732 | tf_op jit(solution)/shard_map/while
  283.3 9.7 %copy-start.1 = (bf16[256,16,128]{2,1,0:T(8,128)(2,1)S(1)}, bf16[256,16,128]{2,1,0:T(8,128)(2,1)}, u32[]{:S(2)}) copy-start(bf16[256,16,128]{2,1,0:T(8,128)(2,1)} %copy-done) | copy-start | bytes 3145732 | tf_op jit(solution)/shard_map/while
  303.0 9.7 %copy-start.1 = (bf16[256,16,128]{2,1,0:T(8,128)(2,1)S(1)}, bf16[256,16,128]{2,1,0:T(8,128)(2,1)}, u32[]{:S(2)}) copy-start(bf16[256,16,128]{2,1,0:T(8,128)(2,1)} %copy-done) | copy-start | bytes 3145732 | tf_op jit(solution)/shard_map/while
  322.8 9.7 %copy-start.1 = (bf16[256,16,128]{2,1,0:T(8,128)(2,1)S(1)}, bf16[256,16,128]{2,1,0:T(8,128)(2,1)}, u32[]{:S(2)}) copy-start(bf16[256,16,128]{2,1,0:T(8,128)(2,1)} %copy-done) | copy-start | bytes 3145732 | tf_op jit(solution)/shard_map/while
  342.5 9.7 %copy-start.1 = (bf16[256,16,128]{2,1,0:T(8,128)(2,1)S(1)}, bf16[256,16,128]{2,1,0:T(8,128)(2,1)}, u32[]{:S(2)}) copy-start(bf16[256,16,128]{2,1,0:T(8,128)(2,1)} %copy-done) | copy-start | bytes 3145732 | tf_op jit(solution)/shard_map/while
  419.5 152.8 %reduce-scatter.5.cloned.1.call-start = ((), (), s32[]{:S(2)}) async-start(), calls=%async_computation.2 | async-start | bytes 10027008 | tf_op jit(solution)/shard_map/reduce_scatter | solution.py:138
  (16 other events, 59.5 us)
Sparse Core Ops, SparseCore 0:
  419.6 77.8 reduce-scatter.6
  500.0 72.2 reduce-scatter.4
